TPU v7x, 32 devices: a whole 2x2x4 slice. The times are simulated.
32 devices in a mesh: rep: 4 (over y, core), shard: 8 (over z, x).
Axes of the slice: x: 2, y: 2, z: 4, core: 2. Of those that a mesh axis runs over, the one named last changes fastest.
Arguments:
- grad_kv: bfloat16 [4, 2, 8192, 1024], P('rep', None, 'shard'), may hold values from -24 to 24
- error_kv: float32 [4, 2, 8192, 1024], P('rep', None, 'shard'), may hold values from -12 to 12
- basis_kv: float32 [2, 1024, 64], replicated, may hold values from -6 to 6
Outputs:
- update_kv: bfloat16 [2, 8192, 1024], P(None, 'shard')
- new_error: float32 [4, 2, 8192, 1024], P('rep', None, 'shard')
- basis_next: float32 [2, 1024, 64], replicated
All inputs are finite; a program needn't handle non-finite values.
Results may differ from a plain program's by a relative error of at most 0.001.
Values sent between devices are 32-bit elements; how exact they have to be, the bound alone decides.
No kernel may reach another device: no remote copies, remote signals or barrier semaphores. Data moves between devices by JAX's collectives and lax.ppermute only.
A program may use at most 64 MiB of HBM per device.

v0:
```python
import jax
import jax.numpy as jnp
from jax import lax
from jax.sharding import PartitionSpec as P


def orthogonal(left, gram):
    chol = jnp.linalg.cholesky(gram)
    ortho = lax.linalg.triangular_solve(chol, left, left_side=False, lower=True, transpose_a=True)
    return (chol, ortho)


def on_device(grad_kv, error_kv, basis_kv):
    highest = lax.Precision.HIGHEST
    replicas = lax.axis_size("rep")
    merged = grad_kv[0].astype(jnp.float32) + error_kv[0]
    local_left = jnp.einsum("mrc,mck->mrk", merged, basis_kv, precision=highest)
    left = lax.psum(local_left, "rep") / replicas
    local_gram = jnp.einsum("mrk,mrl->mkl", left, left, precision=highest)
    gram = lax.psum(local_gram, "shard")
    chol, ortho = orthogonal(left, gram)
    local_right = jnp.einsum("mrc,mrk->mck", merged, ortho, precision=highest)
    shares = lax.psum_scatter(local_right, "shard", scatter_dimension=1, tiled=True)
    shares = lax.psum(shares, "rep")
    right = lax.all_gather(shares, "shard", axis=1, tiled=True) / replicas
    approx = jnp.einsum("mrk,mck->mrc", ortho, right, precision=highest)
    new_error = (merged - approx)[None]
    return (approx.astype(jnp.bfloat16), new_error, right)


def solution(mesh):
    placed = (P("rep", None, "shard", None), P("rep", None, "shard", None), P())
    return jax.shard_map(
        on_device,
        mesh=mesh,
        in_specs=placed,
        out_specs=(P(None, "shard", None), P("rep", None, "shard", None), P()),
        check_vma=False,
    )
```

profile of v0, /device:TPU:0, one launch (start us, length us, event | category | flops | bytes accessed | tf_op | source)
XLA Modules:
  0.0 273.9 jit_solution(2722910858909565346)
XLA Ops:
  7.2 0.0 copy-start
  7.2 0.0 all-reduce.3.cloned.1.call-start
  7.2 1.0 copy-done
  8.2 12.4 %fusion.2 = f32[2,1024,64]{1,2,0:T(8,128)} fusion(f32[2,1024,64]{1,2,0:T(8,128)S(1)} %copy-done, f32[1,2,1024,1024]{3,2,1,0:T(8,128)} %param.4, bf16[1,2,1024,1024]{3,2,1,0:T(8,128)(2,1)} %param.3), kind=kOutput, calls=%fused_computation.3 | convolution fusion | flops 1614807040 | bytes 13631488 | tf_op jit(solution)/shard_map/mrc,mck->mrk/dot_general | solution.py:17
  20.6 0.0 all-reduce.3.cloned.1.call-update
  20.6 0.0 reduce-scatter.2.cloned.1.call-start
  20.7 36.2 %all-reduce.3.cloned.1.call-done = f32[2,1024,64]{1,2,0:T(8,128)} async-done(((f32[2,1024,64]{1,2,0:T(8,128)}), f32[2,1024,64]{1,2,0:T(8,128)}) %all-reduce.3.cloned.1.call-update) | async-done | bytes 524304 | tf_op jit(solution)/shard_map/psum | solution.py:18
  56.9 1.9 fusion.7
  58.8 37.5 %psum.22 = f32[2,64,64]{1,2,0:T(8,128)S(1)} all-reduce(f32[2,64,64]{1,2,0:T(8,128)S(1)} %fusion.7), channel_id=1, replica_groups=mesh['rep'=4,'shard'=8] {'shard'}, use_global_device_ids=true, to_apply=%region_1.0 | all-reduce | flops 8192 | bytes 65536 | tf_op jit(solution)/shard_map/psum | solution.py:20
  96.3 0.1 copy.10
  96.4 11.7 %custom-call.7 = f32[2,64,64]{2,1,0:T(8,128)S(1)} custom-call(f32[2,64,64]{2,1,0:T(8,128)S(1)} %fusion.12), custom_call_target="Cholesky" | custom-call | tf_op jit(solution)/shard_map/jit(cholesky)/cholesky | solution.py:8
  108.2 0.1 compare_reduce_fusion
  108.3 0.1 select_bitcast_fusion
  108.4 9.8 %custom-call.8 = f32[2,1,64,64]{2,3,1,0:T(8,128)S(1)} custom-call(f32[2,1,64,64]{3,2,1,0:T(8,128)S(1)} %select_bitcast_fusion), custom_call_target="InvertDiagBlocksLowerTriangular" | custom-call | tf_op jit(solution)/shard_map/triangular_solve | solution.py:9
  118.2 1.7 fusion.5
  119.9 9.6 %fusion = f32[2,1024,64]{1,2,0:T(8,128)} fusion(f32[2,1024,64]{1,2,0:T(8,128)S(1)} %fusion.5, f32[1,2,1024,1024]{3,2,1,0:T(8,128)} %param.4, bf16[1,2,1024,1024]{3,2,1,0:T(8,128)(2,1)} %param.3), kind=kOutput, calls=%fused_computation.1 | convolution fusion | flops 1614807040 | bytes 13631488 | tf_op jit(solution)/shard_map/mrc,mrk->mck/dot_general | solution.py:22
  129.6 0.0 reduce-scatter.2.cloned.1.call-update
  129.6 0.0 all-reduce.5.cloned.1.call-start
  129.6 59.7 %reduce-scatter.2.cloned.1.call-done = f32[2,128,64]{1,2,0:T(8,128)} async-done(((f32[2,1024,64]{1,2,0:T(8,128)}), f32[2,128,64]{1,2,0:T(8,128)}) %reduce-scatter.2.cloned.1.call-update) | async-done | bytes 65552 | tf_op jit(solution)/shard_map/reduce_scatter | solution.py:23
  189.4 0.0 all-reduce.5.cloned.1.call-update
  189.4 32.9 %all-reduce.5.cloned.1.call-done = f32[2,128,64]{1,2,0:T(8,128)} async-done(((f32[2,128,64]{1,2,0:T(8,128)}), f32[2,128,64]{1,2,0:T(8,128)}) %all-reduce.5.cloned.1.call-update) | async-done | bytes 65552 | tf_op jit(solution)/shard_map/psum | solution.py:24
  222.3 31.8 %all_gather.3 = f32[2,1024,64]{1,2,0:T(8,128)S(1)} all-gather(f32[2,128,64]{1,2,0:T(8,128)} %all-reduce.5.cloned.1.call-done), channel_id=1, replica_groups=mesh['rep'=4,'shard'=8] {'shard'}, dimensions={1}, use_global_device_ids=true | all-gather | bytes 589824 | tf_op jit(solution)/shard_map/all_gather | solution.py:25
  254.1 0.0 copy-start.1
  254.1 13.3 %fusion.4 = (f32[1,2,1024,1024]{3,2,1,0:T(8,128)}, bf16[2,1024,1024]{2,1,0:T(8,128)(2,1)}) fusion(f32[1,2,1024,1024]{3,2,1,0:T(8,128)} %param.4, bf16[1,2,1024,1024]{3,2,1,0:T(8,128)(2,1)} %param.3, f32[2,1024,64]{1,2,0:T(8,128)S(1)} %fusion.5, f32[2,1024,64]{1,2,0:T(8,128)S(1)} %broadcast_multiply_fusion), kind=kOutput, calls=%fused_computation.5 | convolution fusion | flops 1619001344 | bytes 26214400 | tf_op jit(solution)/shard_map/mrk,mck->mrc/dot_general | solution.py:26
  267.4 0.0 copy-done.1
  (5 shorter events, 0.1 us)
Async XLA Ops:
  7.2 1.0 copy-start
  7.2 49.8 %all-reduce.3.cloned.1.call-start = ((), (), s32[]{:S(2)}) async-start(), calls=%async_computation.1 | async-start | bytes 1048576 | tf_op jit(solution)/shard_map/psum | solution.py:18
  20.6 168.7 %reduce-scatter.2.cloned.1.call-start = ((), (), s32[]{:S(2)}) async-start(), calls=%async_computation.2 | async-start | bytes 589824 | tf_op jit(solution)/shard_map/reduce_scatter | solution.py:23
  129.6 92.7 %all-reduce.5.cloned.1.call-start = ((), (), s32[]{:S(2)}) async-start(), calls=%async_computation.3 | async-start | bytes 131072 | tf_op jit(solution)/shard_map/psum | solution.py:24
  254.1 13.3 %copy-start.1 = (f32[2,1024,64]{1,2,0:T(8,128)}, f32[2,1024,64]{1,2,0:T(8,128)S(1)}, u32[]{:S(2)}) copy-start(f32[2,1024,64]{1,2,0:T(8,128)S(1)} %broadcast_multiply_fusion) | copy-start | bytes 1572868
Sparse Core Ops, SparseCore 0:
  20.8 36.1 all-reduce.2
  129.7 59.6 reduce-scatter.1
  191.7 30.5 all-reduce.4
where the time goes:
time: 274 us
  waiting for transfers between devices  129 us (47%)
  blocking collectives  69.3 us (25%)
  matrix products  38.9 us (14%)
  other arithmetic  21.9 us (8%)
  between operations  13.8 us (5%)
    reduce_scatter x1, waiting for transfers between devices, on_device(): lax.psum_scatter(local_right, 'shard', scatter_dimension=1, tiled=True)  59.7 us
    psum x1, blocking collectives, on_device(): gram = lax.psum(local_gram, 'shard')  37.5 us
    psum x1, waiting for transfers between devices, on_device(): left = lax.psum(local_left, 'rep') / replicas  36.2 us
    psum x1, waiting for transfers between devices, on_device(): shares = lax.psum(shares, 'rep')  32.9 us
    all_gather x1, blocking collectives, on_device(): right = lax.all_gather(shares, 'shard', axis=1, tiled=True) / replicas  31.8 us
    dot_general x1, matrix products, on_device(): approx = jnp.einsum('mrk,mck->mrc', ortho, right, precision=highest)  13.3 us
    dot_general x1, matrix products, on_device(): local_left = jnp.einsum('mrc,mck->mrk', merged, basis_kv, precision=highest)  12.4 us
    another operation x4, other arithmetic, orthogonal(): chol = jnp.linalg.cholesky(gram)  11.9 us
  transfers between devices with their start and end apart: 3, of which 3 were waited for; matrix products, arithmetic and copies ran while one was open for 0% of the time, Pallas kernels for 0%

commit v1 on v0

--- a/solution.py
+++ b/solution.py
@@ -17,7 +17,9 @@
     local_left = jnp.einsum("mrc,mck->mrk", merged, basis_kv, precision=highest)
     left = lax.psum(local_left, "rep") / replicas
     local_gram = jnp.einsum("mrk,mrl->mkl", left, left, precision=highest)
-    gram = lax.psum(local_gram, "shard")
+    gram = local_gram
+    for hop in (1, 2, 4):
+        gram = gram + lax.ppermute(gram, "shard", [(dev, dev ^ hop) for dev in range(8)])
     chol, ortho = orthogonal(left, gram)
     local_right = jnp.einsum("mrc,mrk->mck", merged, ortho, precision=highest)
     shares = lax.psum_scatter(local_right, "shard", scatter_dimension=1, tiled=True)

time: 274 us -> 255 us (0.931)
  blocking collectives: 69.3 us -> 31.8 us
  waiting for transfers between devices: 129 us -> 141 us
  starting transfers between devices: 0.12 us -> 6.3 us
    psum x1 -> x0, blocking collectives: 37.5 us -> none  [on_device(): gram = lax.psum(local_gram, 'shard')]
    ppermute x0 -> x3, waiting for transfers between devices: none -> 7.81 us  [on_device(): lax.ppermute(gram, 'shard', [(dev, dev ^ hop) for dev in range(8)])]
    ppermute x0 -> x3, starting transfers between devices: none -> 6.18 us  [on_device(): lax.ppermute(gram, 'shard', [(dev, dev ^ hop) for dev in range(8)])]
    reduce_scatter x1, waiting for transfers between devices: 59.7 us -> 64 us  [on_device(): lax.psum_scatter(local_right, 'shard', scatter_dimension=1, tiled=True)]
  transfers between devices with their start and end apart: 3 -> 6, of which waited for: 3 -> 6; matrix products, arithmetic and copies ran while one was open for 0% -> 0% of each run, Pallas kernels for 0% -> 0%
where the time goes in v1:
time: 255 us
  waiting for transfers between devices  141 us (55%)
  matrix products  38.9 us (15%)
  blocking collectives  31.8 us (12%)
  other arithmetic  21.9 us (9%)
  between operations  13.8 us (5%)
  starting transfers between devices  6.3 us (2%)
    reduce_scatter x1, waiting for transfers between devices, on_device(): lax.psum_scatter(local_right, 'shard', scatter_dimension=1, tiled=True)  64 us
    psum x1, waiting for transfers between devices, on_device(): left = lax.psum(local_left, 'rep') / replicas  36.3 us
    psum x1, waiting for transfers between devices, on_device(): shares = lax.psum(shares, 'rep')  32.8 us
    all_gather x1, blocking collectives, on_device(): right = lax.all_gather(shares, 'shard', axis=1, tiled=True) / replicas  31.8 us
    dot_general x1, matrix products, on_device(): approx = jnp.einsum('mrk,mck->mrc', ortho, right, precision=highest)  13.3 us
    dot_general x1, matrix products, on_device(): local_left = jnp.einsum('mrc,mck->mrk', merged, basis_kv, precision=highest)  12.4 us
    another operation x4, other arithmetic, orthogonal(): chol = jnp.linalg.cholesky(gram)  11.9 us
    another operation x3, other arithmetic, orthogonal(): lax.linalg.triangular_solve(chol, left, left_side=False, lower=True, tran...  9.92 us
  transfers between devices with their start and end apart: 6, of which 6 were waited for; matrix products, arithmetic and copies ran while one was open for 0% of the time, Pallas kernels for 0%

profile of v1, /device:TPU:0, one launch (start us, length us, event | category | flops | bytes accessed | tf_op | source)
XLA Modules:
  0.0 254.7 jit_solution(3730519452871555994)
XLA Ops:
  7.2 0.0 copy-start
  7.2 0.0 all-reduce.3.cloned.1.call-start
  7.2 1.0 copy-done
  8.2 12.4 %fusion.2 = f32[2,1024,64]{1,2,0:T(8,128)} fusion(f32[2,1024,64]{1,2,0:T(8,128)S(1)} %copy-done, f32[1,2,1024,1024]{3,2,1,0:T(8,128)} %param.4, bf16[1,2,1024,1024]{3,2,1,0:T(8,128)(2,1)} %param.3), kind=kOutput, calls=%fused_computation.3 | convolution fusion | flops 1614807040 | bytes 13631488 | tf_op jit(solution)/shard_map/mrc,mck->mrk/dot_general | solution.py:17
  20.6 0.0 all-reduce.3.cloned.1.call-update
  20.6 0.0 reduce-scatter.2.cloned.1.call-start
  20.7 36.3 %all-reduce.3.cloned.1.call-done = f32[2,1024,64]{1,2,0:T(8,128)} async-done(((f32[2,1024,64]{1,2,0:T(8,128)}), f32[2,1024,64]{1,2,0:T(8,128)}) %all-reduce.3.cloned.1.call-update) | async-done | bytes 524304 | tf_op jit(solution)/shard_map/psum | solution.py:18
  56.9 1.9 fusion.7
  58.8 1.5 collective-permute-start
  60.3 2.8 %collective-permute-done = f32[2,64,64]{1,2,0:T(8,128)S(1)} collective-permute-done((f32[2,64,64]{1,2,0:T(8,128)S(1)}, f32[2,64,64]{1,2,0:T(8,128)S(1)}, u32[]{:S(2)}, u32[]{:S(2)}) %collective-permute-start) | collective-permute-done | bytes 32800 | tf_op jit(solution)/shard_map/ppermute | solution.py:22
  63.2 1.6 collective-permute-start.1
  64.7 2.8 %collective-permute-done.1 = f32[2,64,64]{1,2,0:T(8,128)S(1)} collective-permute-done((f32[2,64,64]{1,2,0:T(8,128)S(1)}, f32[2,64,64]{1,2,0:T(8,128)S(1)}, u32[]{:S(2)}, u32[]{:S(2)}) %collective-permute-start.1) | collective-permute-done | bytes 32800 | tf_op jit(solution)/shard_map/ppermute | solution.py:22
  67.5 3.1 %collective-permute-start.2 = (f32[2,64,64]{1,2,0:T(8,128)S(1)}, f32[2,64,64]{1,2,0:T(8,128)S(1)}, u32[]{:S(2)}, u32[]{:S(2)}) collective-permute-start(f32[2,64,64]{1,2,0:T(8,128)S(1)} %add.35), channel_id=1, source_target_pairs={{0,4},{1,5},{2,6},{3,7},{4,0},{5,1},{6,2},{7,3},{8,12},{9,13},{10,... | collective-permute-start | bytes 98312 | tf_op jit(solution)/shard_map/ppermute | solution.py:22
  70.6 2.2 collective-permute-done.2
  72.9 0.1 copy.12
  73.0 11.7 %custom-call.7 = f32[2,64,64]{2,1,0:T(8,128)S(1)} custom-call(f32[2,64,64]{2,1,0:T(8,128)S(1)} %fusion.12), custom_call_target="Cholesky" | custom-call | tf_op jit(solution)/shard_map/jit(cholesky)/cholesky | solution.py:8
  84.7 0.1 compare_reduce_fusion
  84.9 0.1 select_bitcast_fusion
  84.9 9.8 %custom-call.8 = f32[2,1,64,64]{2,3,1,0:T(8,128)S(1)} custom-call(f32[2,1,64,64]{3,2,1,0:T(8,128)S(1)} %select_bitcast_fusion), custom_call_target="InvertDiagBlocksLowerTriangular" | custom-call | tf_op jit(solution)/shard_map/triangular_solve | solution.py:9
  94.8 1.7 fusion.5
  96.4 9.6 %fusion = f32[2,1024,64]{1,2,0:T(8,128)} fusion(f32[2,1024,64]{1,2,0:T(8,128)S(1)} %fusion.5, f32[1,2,1024,1024]{3,2,1,0:T(8,128)} %param.4, bf16[1,2,1024,1024]{3,2,1,0:T(8,128)(2,1)} %param.3), kind=kOutput, calls=%fused_computation.1 | convolution fusion | flops 1614807040 | bytes 13631488 | tf_op jit(solution)/shard_map/mrc,mrk->mck/dot_general | solution.py:24
  106.1 0.0 reduce-scatter.2.cloned.1.call-update
  106.1 0.0 all-reduce.5.cloned.1.call-start
  106.2 64.0 %reduce-scatter.2.cloned.1.call-done = f32[2,128,64]{1,2,0:T(8,128)} async-done(((f32[2,1024,64]{1,2,0:T(8,128)}), f32[2,128,64]{1,2,0:T(8,128)}) %reduce-scatter.2.cloned.1.call-update) | async-done | bytes 65552 | tf_op jit(solution)/shard_map/reduce_scatter | solution.py:25
  170.2 0.0 all-reduce.5.cloned.1.call-update
  170.2 32.8 %all-reduce.5.cloned.1.call-done = f32[2,128,64]{1,2,0:T(8,128)} async-done(((f32[2,128,64]{1,2,0:T(8,128)}), f32[2,128,64]{1,2,0:T(8,128)}) %all-reduce.5.cloned.1.call-update) | async-done | bytes 65552 | tf_op jit(solution)/shard_map/psum | solution.py:26
  203.0 31.8 %all_gather.3 = f32[2,1024,64]{1,2,0:T(8,128)S(1)} all-gather(f32[2,128,64]{1,2,0:T(8,128)} %all-reduce.5.cloned.1.call-done), channel_id=1, replica_groups=mesh['rep'=4,'shard'=8] {'shard'}, dimensions={1}, use_global_device_ids=true | all-gather | bytes 589824 | tf_op jit(solution)/shard_map/all_gather | solution.py:27
  234.9 0.0 copy-start.1
  234.9 13.3 %fusion.4 = (f32[1,2,1024,1024]{3,2,1,0:T(8,128)}, bf16[2,1024,1024]{2,1,0:T(8,128)(2,1)}) fusion(f32[1,2,1024,1024]{3,2,1,0:T(8,128)} %param.4, bf16[1,2,1024,1024]{3,2,1,0:T(8,128)(2,1)} %param.3, f32[2,1024,64]{1,2,0:T(8,128)S(1)} %fusion.5, f32[2,1024,64]{1,2,0:T(8,128)S(1)} %broadcast_multiply_fusion), kind=kOutput, calls=%fused_computation.5 | convolution fusion | flops 1619001344 | bytes 26214400 | tf_op jit(solution)/shard_map/mrk,mck->mrc/dot_general | solution.py:28
  248.2 0.0 copy-done.1
  (8 shorter events, 0.1 us)
Async XLA Ops:
  7.2 1.0 copy-start
  7.2 49.8 %all-reduce.3.cloned.1.call-start = ((), (), s32[]{:S(2)}) async-start(), calls=%async_computation.1 | async-start | bytes 1048576 | tf_op jit(solution)/shard_map/psum | solution.py:18
  20.6 149.5 %reduce-scatter.2.cloned.1.call-start = ((), (), s32[]{:S(2)}) async-start(), calls=%async_computation.2 | async-start | bytes 589824 | tf_op jit(solution)/shard_map/reduce_scatter | solution.py:25
  58.8 4.3 %collective-permute-start = (f32[2,64,64]{1,2,0:T(8,128)S(1)}, f32[2,64,64]{1,2,0:T(8,128)S(1)}, u32[]{:S(2)}, u32[]{:S(2)}) collective-permute-start(f32[2,64,64]{1,2,0:T(8,128)S(1)} %fusion.7), channel_id=1, source_target_pairs={{0,1},{1,0},{2,3},{3,2},{4,5},{5,4},{6,7},{7,6},{8,9},{9,8},{10,11... | collective-permute-start | bytes 98312 | tf_op jit(solution)/shard_map/ppermute | solution.py:22
  63.2 4.3 %collective-permute-start.1 = (f32[2,64,64]{1,2,0:T(8,128)S(1)}, f32[2,64,64]{1,2,0:T(8,128)S(1)}, u32[]{:S(2)}, u32[]{:S(2)}) collective-permute-start(f32[2,64,64]{1,2,0:T(8,128)S(1)} %add.34), channel_id=1, source_target_pairs={{0,2},{1,3},{2,0},{3,1},{4,6},{5,7},{6,4},{7,5},{8,10},{9,11},{10,... | collective-permute-start | bytes 98312 | tf_op jit(solution)/shard_map/ppermute | solution.py:22
  67.5 5.3 %collective-permute-start.2 = (f32[2,64,64]{1,2,0:T(8,128)S(1)}, f32[2,64,64]{1,2,0:T(8,128)S(1)}, u32[]{:S(2)}, u32[]{:S(2)}) collective-permute-start(f32[2,64,64]{1,2,0:T(8,128)S(1)} %add.35), channel_id=1, source_target_pairs={{0,4},{1,5},{2,6},{3,7},{4,0},{5,1},{6,2},{7,3},{8,12},{9,13},{10,... | collective-permute-start | bytes 98312 | tf_op jit(solution)/shard_map/ppermute | solution.py:22
  106.1 96.9 %all-reduce.5.cloned.1.call-start = ((), (), s32[]{:S(2)}) async-start(), calls=%async_computation.3 | async-start | bytes 131072 | tf_op jit(solution)/shard_map/psum | solution.py:26
  234.9 13.3 %copy-start.1 = (f32[2,1024,64]{1,2,0:T(8,128)}, f32[2,1024,64]{1,2,0:T(8,128)S(1)}, u32[]{:S(2)}) copy-start(f32[2,1024,64]{1,2,0:T(8,128)S(1)} %broadcast_multiply_fusion) | copy-start | bytes 1572868
Sparse Core Ops, SparseCore 0:
  20.8 36.1 all-reduce.2
  106.2 63.8 reduce-scatter.1
  172.5 30.5 all-reduce.4
